TPU v7x, 32 devices: a whole 2x2x4 slice. The times are simulated.
32 devices in a mesh: groups: 2 (over y), date: 4 (over z), row: 2 (over core), col: 2 (over x).
Axes of the slice: x: 2, y: 2, z: 4, core: 2. Of those that a mesh axis runs over, the one named last changes fastest.
Arguments:
- pixels: bfloat16 [8, 2, 13, 384, 192], P(('groups', 'date'), None, None, 'row', 'col'), parts along dimension 0, may hold values from -6 to 6
- w_stem: bfloat16 [64, 13, 7, 7], replicated, may hold values from -0.25 to 0.25
- w_head: float32 [64, 128], replicated, may hold values from -0.75 to 0.75
- pool_grid: int32 [192, 96], P('row', 'col'), may hold values from 0 to 71, as said below
- neg_index: int32 [8, 2, 24, 12, 128], P(('groups', 'date'), None, 'row', 'col'), parts along dimension 0, may hold values from 0 to 143
- key_date: int32 [4], replicated, may hold values from 0 to 3, as said below
Outputs:
- anchor_loss: float32 [8, 2, 24, 12], P(('groups', 'date'), None, 'row', 'col'), parts along dimension 0
- grad_stem: float32 [128, 13, 7, 7], P('groups'), parts along dimension 0
- grad_head: float32 [128, 128], P('groups'), parts along dimension 0
There are 2 independent parts, one for each index of `groups`. A program takes and returns all parts, laid end to end along the dimension named above; an argument that names none is the same for every part. Nothing has to cross between parts.
Inputs may be any that keep to these rules, and one draw needn't show every extreme that they name: `pool_grid`: cell numbers are local to a device block of 96 x 48 stem outputs; every block names each of its 72 cells at least once. `neg_index`: entry k names key k = t * 72 + c of the same block: cell c of tile t on the paired date. Following d to key_date[d] runs once through all 4 dates and back; no date is its own key date.
All inputs are finite; a program needn't handle non-finite values.
Results may differ from a plain program's by a relative error of at most 0.0052.
Values may be sent and summed in bfloat16 or wider, within the bound.
A program may use at most 128 MiB of HBM per device.

v0:
```python
import math

import jax
import jax.numpy as jnp
from jax import lax
from jax.sharding import PartitionSpec as P

CELL = 8


TEMP = 0.2
EPS = 1e-06


def padded_2(array, sides, width):
    for axis, dim in sides:
        peers, length = (lax.axis_size(axis), array.shape[dim])
        up = [(i, (i + 1) % peers) for i in range(peers - 1)]
        down = [(j, i) for i, j in up]
        last = lax.slice_in_dim(array, length - width, length, axis=dim)
        initial = lax.slice_in_dim(array, 0, width, axis=dim)
        before = lax.ppermute(last, axis, up)
        after = lax.ppermute(initial, axis, down)
        array = jnp.concatenate([before, array, after], axis=dim)
    return array


def stem_conv(padded, w_stem):
    return lax.conv_general_dilated(
        padded,
        w_stem,
        (2, 2),
        "VALID",
        dimension_numbers=("NCHW", "OIHW", "NCHW"),
        preferred_element_type=jnp.float32,
    )


def weight_term(padded, slope_low):
    left_side = jnp.transpose(padded, (1, 0, 2, 3))
    right_side = jnp.transpose(slope_low, (1, 0, 2, 3))
    result = lax.conv_general_dilated(
        left_side,
        right_side,
        (1, 1),
        "VALID",
        rhs_dilation=(2, 2),
        dimension_numbers=("NCHW", "OIHW", "NCHW"),
        preferred_element_type=jnp.float32,
    )
    return jnp.transpose(result, (1, 0, 2, 3))


def local(pixels, w_stem, w_head, pool_grid, neg_index, key_date):
    tile_data = pixels[0]
    height = tile_data.shape[2]
    width = tile_data.shape[3]
    extended = padded_2(tile_data, (("row", 2), ("col", 3)), 3)
    padded = extended[:, :, : height + 5, : width + 5]
    stem_out = stem_conv(padded, w_stem)
    tiles, channels, feat_rows, feat_cols = stem_out.shape
    hidden = (
        jnp.maximum(stem_out, 0.0)
        .astype(jnp.bfloat16)
        .reshape(tiles, channels, feat_rows * feat_cols)
    )
    cells = feat_rows // CELL * (feat_cols // CELL)
    anchors = tiles * cells
    grid_flat = pool_grid.reshape(-1)
    member = grid_flat[:, None] == jnp.arange(cells, dtype=jnp.int32)[None, :]
    counts = jnp.sum(member.astype(jnp.float32), axis=0)
    cell_sums = jnp.einsum(
        "tcp,pk->tkc", hidden, member.astype(jnp.bfloat16), preferred_element_type=jnp.float32
    )
    pooled = (cell_sums / counts[None, :, None]).reshape(anchors, channels)
    project = jnp.dot(pooled, w_head, precision=lax.Precision.HIGHEST)
    length = jnp.sqrt(jnp.sum(project * project, axis=-1, keepdims=True) + EPS)
    embed = project / length
    dates = lax.axis_size("date")
    date_here = lax.axis_index("date")
    date_ids = jnp.arange(dates, dtype=jnp.int32)
    target_date = jnp.sum(jnp.where(date_ids == date_here, key_date, 0))
    source_date = jnp.sum(jnp.where(key_date == date_here, date_ids, 0))
    all_keys = lax.all_gather(embed[None], "date", axis=0, tiled=True)
    key_rows = lax.dynamic_index_in_dim(all_keys, target_date, 0, keepdims=False)
    scores = jnp.dot(embed, key_rows.T, precision=lax.Precision.HIGHEST) / TEMP
    neg_rows = neg_index[0].reshape(anchors, -1)
    negative = jnp.take_along_axis(scores, neg_rows, axis=1)
    positive = jnp.diagonal(scores)
    denominator = jnp.exp(positive) + jnp.sum(jnp.exp(negative), axis=1)
    losses = jnp.log(denominator) - positive
    anchor_loss = losses.reshape(1, tiles, feat_rows // CELL, feat_cols // CELL)
    scale = 1.0 / math.sqrt(dates * anchors * lax.axis_size("row") * lax.axis_size("col"))
    d_pos = scale * (jnp.exp(positive) / denominator - 1.0)
    d_neg = scale * jnp.exp(negative) / denominator[:, None]
    arange_rows = jnp.arange(anchors, dtype=jnp.int32)
    d_scores = (
        jnp.zeros((anchors, anchors), jnp.float32).at[arange_rows[:, None], neg_rows].add(d_neg)
    )
    d_scores = d_scores.at[arange_rows, arange_rows].add(d_pos) / TEMP
    grad_anchor = jnp.dot(d_scores, key_rows, precision=lax.Precision.HIGHEST)
    grad_keys = jnp.dot(d_scores.T, embed, precision=lax.Precision.HIGHEST)
    all_grads = lax.all_gather(grad_keys[None], "date", axis=0, tiled=True)
    returned = lax.dynamic_index_in_dim(all_grads, source_date, 0, keepdims=False)
    grad_embed = grad_anchor + returned
    grad_project = (
        grad_embed - embed * jnp.sum(embed * grad_embed, axis=-1, keepdims=True)
    ) / length
    head_term = jnp.dot(pooled.T, grad_project, precision=lax.Precision.HIGHEST)
    grad_pooled = jnp.dot(grad_project, w_head.T, precision=lax.Precision.HIGHEST)
    per_cell = grad_pooled.reshape(tiles, cells, channels) / counts[None, :, None]
    cell_major = jnp.transpose(per_cell, (0, 2, 1))
    spread = jnp.take(cell_major, grid_flat, axis=2)
    spread = spread.reshape(tiles, channels, feat_rows, feat_cols)
    slope_low = jnp.where(stem_out > 0, spread, 0.0).astype(jnp.bfloat16)
    stem_term = weight_term(padded, slope_low)
    grad_stem, grad_head = lax.psum((stem_term, head_term), ("date", "row", "col"))
    return (anchor_loss, grad_stem, grad_head)


def solution(mesh):
    placed = (
        P(("groups", "date"), None, None, "row", "col"),
        P(),
        P(),
        P("row", "col"),
        P(("groups", "date"), None, "row", "col", None),
        P(),
    )
    return jax.shard_map(
        local,
        mesh=mesh,
        in_specs=placed,
        out_specs=(
            P(("groups", "date"), None, "row", "col"),
            P("groups", None, None, None),
            P("groups", None),
        ),
        check_vma=False,
    )
```

profile of v0, /device:TPU:0, one launch (start us, length us, event | category | flops | bytes accessed | tf_op | source)
XLA Modules:
  0.0 792.7 jit_solution(11506925040963136276)
XLA Ops:
  7.3 16.0 %copy.165 = bf16[1,2,13,192,96]{2,1,4,3,0:T(2,128)(2,1)} copy(bf16[1,2,13,192,96]{4,3,2,1,0:T(8,128)(2,1)} %param.6) | data formatting | bytes 1916928 | tf_op args[0]
  23.3 1.2 fusion.42
  24.6 2.4 collective-permute-start
  27.1 1.3 collective-permute-start.1
  30.2 0.6 fusion.37
  30.9 0.6 select_bitcast_fusion
  31.9 2.2 pad_maximum_fusion.3
  34.1 4.2 collective-permute-start.2
  38.3 1.5 collective-permute-start.3
  42.5 0.6 reshape_squeeze.6
  44.4 1.3 collective-permute-done.2
  45.7 4.4 collective-permute-done.3
  50.2 0.7 copy-done.8
  50.9 42.7 %fusion.57 = bf16[13,198,2,102]{0,2,3,1:T(2,128)(2,1)} fusion(bf16[2,13,198,3]{1,0,3,2:T(2,128)(2,1)S(1)} %collective-permute-done.3, bf16[2,13,3,96]{1,0,3,2:T(2,128)(2,1)S(1)} %copy.169, bf16[2,13,192,96]{1,0,3,2:T(2,128)(2,1)} %bitcast.93, bf16[2,13,3,96]{1,0,3,2:T(2,128)(2,1)S(1)} %copy.168, bf16[2,13,198,3]{1,0,3,2:T(2,128)(2,1)S(1)} %collective-permute-done.2), kind=kLoop, calls=%fused_computation.87 | loop fusion | flops 2100384 | bytes 2100384 | tf_op jit(solution)/shard_map/concatenate | solution.py:24
  93.6 21.6 %copy.189 = bf16[13,198,2,102]{1,2,3,0:T(2,128)(2,1)S(1)} copy(bf16[13,198,2,102]{0,2,3,1:T(2,128)(2,1)} %fusion.57) | data formatting | bytes 2100384
  115.2 1.4 pad.clone
  116.6 0.4 slice.30
  117.0 2.5 fusion.2
  119.5 19.4 %copy.171 = bf16[13,198,2,8,20]{0,3,2,4,1:T(8,128)(2,1)} copy(bf16[13,198,2,8,20]{1,2,4,3,0:T(2,128)(2,1)S(1)} %fusion.2) | data formatting | bytes 3294720 | tf_op jit(solution)/shard_map/conv_general_dilated | solution.py:29
  139.0 17.7 %maximum_convert_fusion = (bf16[96,16,7,64]{3,1,2,0:T(8,128)(2,1)}, f32[96,16,7,64]{3,1,2,0:T(8,128)}) fusion(pred[16,7]{0,1:T(8,128)(4,1)S(1)} %copy-done.19, bf16[64,13,7,7]{0,3,2,1:T(8,128)(2,1)S(1)} %copy-done, bf16[13,198,2,8,20]{0,3,2,4,1:T(8,128)(2,1)} %copy.171), kind=kOutput, calls=%fused_computation.9 | convolution fusion | flops 879427584 | bytes 5857776 | tf_op jit(solution)/shard_map/conv_general_dilated | solution.py:29
  156.6 4.8 copy.173
  161.5 1.3 slice_bitcast_fusion.1
  162.8 3.6 copy.174
  166.4 6.6 reshape.144
  173.0 1.7 fusion.9
  175.0 0.4 multiply_reduce_fusion.2
  175.5 14.2 %all-gather = f32[576,128]{1,0:T(8,128)S(1)} all-gather(f32[144,128]{1,0:T(8,128)S(1)} %broadcast_divide_fusion), channel_id=2, replica_groups=mesh['groups'=2,'date'=4,'row'=2,'col'=2] {'date'}, dimensions={0}, use_global_device_ids=true | all-gather | bytes 368640 | tf_op jit(solution)/shard_map/all_gather | solution.py:84
  190.0 145.6 %gather_fusion.2 = f32[18432]{0:T(1024)S(1)} fusion(f32[144,144]{1,0:T(8,128)S(1)} %convolution_multiply_fusion, s32[18432]{0:T(1024)S(1)} %bitcast.90), kind=kCustom, calls=%fused_computation.2 | custom fusion | bytes 294912 | tf_op jit(solution)/shard_map/jit(take_along_axis)/gather | solution.py:88
  335.9 2.8 gather_fusion
  338.9 125.0 %scatter_custom_fusion.1 = f32[20736]{0:T(1024)S(1)} fusion(s32[18432]{0:T(1024)} %select_bitcast_fusion, f32[18432]{0:T(1024)S(1)} %fusion.20, f32[]{:T(128)} %constant.33.clone.1), kind=kCustom, calls=%fused_computation.58 | custom fusion | flops 18432 | bytes 83456
  464.0 8.2 %scatter_fusion = f32[144,144]{1,0:T(8,128)S(1)} fusion(f32[144,144]{1,0:T(8,128)S(1)} %reshape.151, s32[144]{0:T(256)S(1)} %bitcast.99, f32[144]{0:T(256)S(1)} %get-tuple-element.35), kind=kCustom, calls=%fused_computation.3 | custom fusion | flops 144 | bytes 2880 | tf_op jit(solution)/shard_map/scatter-add | solution.py:100
  472.2 0.5 fusion.14
  472.7 14.6 %all-gather.1 = f32[576,128]{1,0:T(8,128)S(1)} all-gather(f32[144,128]{1,0:T(8,128)S(1)} %fusion.14), channel_id=3, replica_groups=mesh['groups'=2,'date'=4,'row'=2,'col'=2] {'date'}, dimensions={0}, use_global_device_ids=true | all-gather | bytes 368640 | tf_op jit(solution)/shard_map/all_gather | solution.py:103
  487.3 0.4 multiply_reduce_fusion.1
  487.8 0.8 fusion.45
  488.9 0.7 gather.19
  489.9 12.7 %gather_fusion.1 = bf16[4608,2,64]{2,1,0:T(2,128)(2,1)} fusion(bf16[2,64,72]{1,0,2:T(2,128)(2,1)S(1)} %copy.184, s32[5120]{0:T(1024)S(1)} %pad_clamp_fusion), kind=kCustom, calls=%fused_computation.1 | custom fusion | bytes 2377728 | tf_op jit(solution)/shard_map/jit(_take)/gather | solution.py:113
  502.6 5.0 copy.185
  507.6 3.7 select_compare_fusion
  511.3 5.0 copy.180
  516.3 1.8 select_convert_fusion
  518.1 4.0 copy.186
  522.1 41.4 %fusion.61 = bf16[2,13,198,102]{1,0,3,2:T(2,128)(2,1)S(1)} fusion(bf16[2,13,198,3]{1,0,3,2:T(2,128)(2,1)} %copy-done.8, bf16[2,13,3,96]{1,0,3,2:T(2,128)(2,1)S(1)} %copy-done.6, bf16[2,13,192,96]{1,0,3,2:T(2,128)(2,1)} %bitcast.94, bf16[2,13,3,96]{1,0,3,2:T(2,128)(2,1)S(1)} %copy-done.4, bf16[2,13,198,3]{1,0,3,2:T(2,128)(2,1)} %copy-done.7), kind=kLoop, calls=%bitcast_fusion.2.clone.1 | loop fusion | flops 2100384 | bytes 2100384 | tf_op jit(solution)/shard_map/transpose | solution.py:51
  563.6 130.6 %fusion.43 = f32[64,13,7,7]{0,1,3,2:T(8,128)} fusion(bf16[2,64,96,48]{1,0,3,2:T(2,128)(2,1)S(1)} %copy-done.2, bf16[2,13,198,102]{1,0,3,2:T(2,128)(2,1)S(1)} %fusion.61), kind=kOutput, calls=%fused_computation.84 | convolution fusion | flops 751435776 | bytes 2392912 | tf_op jit(solution)/shard_map/transpose | solution.py:51
  694.2 0.7 copy.187
  694.9 58.3 %psum.15 = f32[64,128]{1,0:T(8,128)} all-reduce(f32[64,128]{1,0:T(8,128)S(1)} %copy-done.13), channel_id=1, replica_groups=mesh['groups'=2,'date'=4,'row'=2,'col'=2] {'date','row','col'}, use_global_device_ids=true, to_apply=%region_9.10 | all-reduce | flops 8192 | bytes 65536 | tf_op jit(solution)/shard_map/psum | solution.py:117
  753.3 30.4 %all-reduce.2.cloned.1.call-done = f32[64,13,7,7]{0,1,3,2:T(8,128)} async-done(((f32[64,13,7,7]{0,1,3,2:T(8,128)}), f32[64,13,7,7]{0,1,3,2:T(8,128)}) %all-reduce.2.cloned.1.call-update) | async-done | bytes 163088 | tf_op jit(solution)/shard_map/psum | solution.py:117
  783.7 1.9 copy.188
  (85 shorter events, 4.2 us)
Async XLA Ops:
  7.2 131.8 %copy-start = (bf16[64,13,7,7]{0,3,2,1:T(8,128)(2,1)S(1)}, bf16[64,13,7,7]{0,3,2,1:T(8,128)(2,1)}, u32[]{:S(2)}) copy-start(bf16[64,13,7,7]{0,3,2,1:T(8,128)(2,1)} %param.7) | copy-start | bytes 244612
  7.2 22.7 %copy-start.21 = (s32[2]{0:T(128)S(1)}, s32[2]{0:T(128)}, u32[]{:S(2)}) copy-start(s32[2]{0:T(128)} %constant.73) | copy-start | bytes 28
  7.2 21.2 %copy-start.15 = (s32[96,48]{0,1:T(8,128)S(1)}, s32[96,48]{0,1:T(8,128)}, u32[]{:S(2)}) copy-start(s32[96,48]{0,1:T(8,128)} %param.9) | copy-start | bytes 55300
  7.2 22.0 %copy-start.9 = (s32[1,2,12,6,128]{4,1,3,2,0:T(2,128)S(1)}, s32[1,2,12,6,128]{4,1,3,2,0:T(2,128)}, u32[]{:S(2)}) copy-start(s32[1,2,12,6,128]{4,1,3,2,0:T(2,128)} %param.10) | copy-start | bytes 221188
  7.2 23.0 %copy-start.22 = (s32[4]{0:T(128)S(1)}, s32[4]{0:T(128)}, u32[]{:S(2)}) copy-start(s32[4]{0:T(128)} %param.11) | copy-start | bytes 52
  7.2 776.4 %all-reduce.2.cloned.1.call-start = ((), (), s32[]{:S(2)}) async-start(), calls=%async_computation | async-start | bytes 802816 | tf_op jit(solution)/shard_map/psum | solution.py:117
  24.6 7.0 collective-permute-start
  27.1 4.6 collective-permute-start.1
  28.6 0.6 copy-start.16
  31.7 18.5 %copy-start.3 = (bf16[2,13,3,96]{1,0,3,2:T(2,128)(2,1)}, bf16[2,13,3,96]{1,0,3,2:T(2,128)(2,1)S(1)}, u32[]{:S(2)}) copy-start(bf16[2,13,3,96]{1,0,3,2:T(2,128)(2,1)S(1)} %copy.168) | copy-start | bytes 44932
  31.9 18.3 %copy-start.5 = (bf16[2,13,3,96]{1,0,3,2:T(2,128)(2,1)}, bf16[2,13,3,96]{1,0,3,2:T(2,128)(2,1)S(1)}, u32[]{:S(2)}) copy-start(bf16[2,13,3,96]{1,0,3,2:T(2,128)(2,1)S(1)} %copy.169) | copy-start | bytes 44932
  34.1 11.7 %collective-permute-start.2 = (bf16[2,13,198,3]{1,0,3,2:T(2,128)(2,1)S(1)}, bf16[2,13,198,3]{1,0,3,2:T(2,128)(2,1)S(1)}, u32[]{:S(2)}, u32[]{:S(2)}) collective-permute-start(bf16[2,13,198,3]{1,0,3,2:T(2,128)(2,1)S(1)} %get-tuple-element.31), channel_id=1, source_target_pairs={{0,1},{2,3},{4,5},{6,7},{8,9},{10,11},{12,13},{14,15},{16,17},{18,... | collective-permute-start | bytes 92672 | tf_op jit(solution)/shard_map/ppermute | solution.py:22
  38.3 11.8 %collective-permute-start.3 = (bf16[2,13,198,3]{1,0,3,2:T(2,128)(2,1)S(1)}, bf16[2,13,198,3]{1,0,3,2:T(2,128)(2,1)S(1)}, u32[]{:S(2)}, u32[]{:S(2)}) collective-permute-start(bf16[2,13,198,3]{1,0,3,2:T(2,128)(2,1)S(1)} %get-tuple-element.32), channel_id=1, source_target_pairs={{1,0},{3,2},{5,4},{7,6},{9,8},{11,10},{13,12},{15,14},{17,16},{19,... | collective-permute-start | bytes 92672 | tf_op jit(solution)/shard_map/ppermute | solution.py:23
  45.7 4.4 copy-start.7
  50.2 0.7 copy-start.8
  119.5 19.5 %copy-start.19 = (pred[16,7]{0,1:T(8,128)(4,1)S(1)}, pred[16,7]{0,1:T(8,128)(4,1)}, u32[]{:S(2)}) copy-start(pred[16,7]{0,1:T(8,128)(4,1)} %constant.85) | copy-start | bytes 340
  161.5 11.5 %copy-start.17 = (s32[4608]{0:T(1024)S(1)}, s32[4608]{0:T(1024)}, u32[]{:S(2)}) copy-start(s32[4608]{0:T(1024)} %copy-done.16) | copy-start | bytes 55300
  162.8 12.2 %copy-start.14 = (f32[64,128]{1,0:T(8,128)S(1)}, f32[64,128]{1,0:T(8,128)}, u32[]{:S(2)}) copy-start(f32[64,128]{1,0:T(8,128)} %param.8) | copy-start | bytes 98308
  190.0 148.7 %copy-start.10 = (s32[144,128]{1,0:T(8,128)S(1)}, s32[144,128]{1,0:T(8,128)}, u32[]{:S(2)}) copy-start(s32[144,128]{1,0:T(8,128)} %reshape_squeeze.6) | copy-start | bytes 221188
  335.8 171.8 %copy-start.11 = (f32[2,12,6]{2,1,0:T(8,128)}, f32[2,12,6]{2,1,0:T(8,128)S(1)}, u32[]{:S(2)}) copy-start(f32[2,12,6]{2,1,0:T(8,128)S(1)} %exponential_reduce_fusion) | copy-start | bytes 1732
  338.7 168.8 %copy-start.20 = (pred[16,7]{0,1:T(8,128)(4,1)S(1)}, pred[16,7]{0,1:T(8,128)(4,1)}, u32[]{:S(2)}) copy-start(pred[16,7]{0,1:T(8,128)(4,1)} %constant.85) | copy-start | bytes 340
  511.3 10.8 %copy-start.4 = (bf16[2,13,3,96]{1,0,3,2:T(2,128)(2,1)S(1)}, bf16[2,13,3,96]{1,0,3,2:T(2,128)(2,1)}, u32[]{:S(2)}) copy-start(bf16[2,13,3,96]{1,0,3,2:T(2,128)(2,1)} %copy-done.3) | copy-start | bytes 44932
  511.3 10.8 %copy-start.6 = (bf16[2,13,3,96]{1,0,3,2:T(2,128)(2,1)S(1)}, bf16[2,13,3,96]{1,0,3,2:T(2,128)(2,1)}, u32[]{:S(2)}) copy-start(bf16[2,13,3,96]{1,0,3,2:T(2,128)(2,1)} %copy-done.5) | copy-start | bytes 44932
  522.1 41.4 %copy-start.2 = (bf16[2,64,96,48]{1,0,3,2:T(2,128)(2,1)S(1)}, bf16[2,64,96,48]{1,0,3,2:T(2,128)(2,1)}, u32[]{:S(2)}) copy-start(bf16[2,64,96,48]{1,0,3,2:T(2,128)(2,1)} %copy.186) | copy-start | bytes 3538948
  563.6 130.6 %copy-start.12 = (f32[2,12,6]{2,1,0:T(8,128)S(1)}, f32[2,12,6]{2,1,0:T(8,128)}, u32[]{:S(2)}) copy-start(f32[2,12,6]{2,1,0:T(8,128)} %copy-done.11) | copy-start | bytes 1732
  563.6 130.6 %copy-start.18 = (f32[1,2,12,6]{3,2,1,0:T(8,128)S(1)}, f32[1,2,12,6]{3,2,1,0:T(8,128)}, u32[]{:S(2)}) copy-start(f32[1,2,12,6]{3,2,1,0:T(8,128)} %gather.19) | copy-start | bytes 1732
  563.6 131.3 %copy-start.13 = (f32[64,128]{1,0:T(8,128)S(1)}, f32[64,128]{1,0:T(8,128)}, u32[]{:S(2)}) copy-start(f32[64,128]{1,0:T(8,128)} %fusion.45) | copy-start | bytes 98308
  563.6 221.9 %copy-start.1 = (bf16[64,13,7,7]{0,3,2,1:T(8,128)(2,1)S(1)}, bf16[64,13,7,7]{0,3,2,1:T(8,128)(2,1)}, u32[]{:S(2)}) copy-start(bf16[64,13,7,7]{0,3,2,1:T(8,128)(2,1)} %param.7) | copy-start | bytes 244612
Sparse Core Ops, SparseCore 0:
  694.3 89.2 all-reduce.1
where the time goes:
time: 799 us; the launch traced here: 793 us
  local copies, waits for them, and re-layouts  258 us (32%)
  other arithmetic  230 us (29%)
  matrix products  153 us (19%)
  blocking collectives  87.2 us (11%)
  waiting for transfers between devices  36.2 us (5%)
  between operations  18.9 us (2%)
  starting transfers between devices  9.44 us (1%)
    gather x3, local copies, waits for them, and re-layouts, local(): negative = jnp.take_along_axis(scores, neg_rows, axis=1)  146 us
    transpose x1, matrix products, weight_term(): return jnp.transpose(result, (1, 0, 2, 3))  131 us
    unnamed x4, other arithmetic  126 us
    psum x1, blocking collectives, local(): lax.psum((stem_term, head_term), ('date', 'row', 'col'))  58.3 us
    concatenate x1, other arithmetic, padded_2(): array = jnp.concatenate([before, array, after], axis=dim)  42.7 us
    transpose x1, other arithmetic, weight_term(): return jnp.transpose(result, (1, 0, 2, 3))  41.4 us
    unnamed x53, local copies, waits for them, and re-layouts  41.3 us
    psum x1, waiting for transfers between devices, local(): lax.psum((stem_term, head_term), ('date', 'row', 'col'))  30.4 us
  transfers between devices with their start and end apart: 5, of which 3 were waited for; matrix products, arithmetic and copies ran while one was open for 1% of the time, Pallas kernels for 0%

commit v1 on v0

v1 whole, which is shorter than its diff:
```python
import functools
import math

import jax
import jax.numpy as jnp
import numpy as np
from jax import lax
from jax.experimental import pallas as pl
from jax.experimental.pallas import tpu as pltpu
from jax.sharding import PartitionSpec as P

CELL = 8
TEMP = 0.2
EPS = 1e-06
STEP = 4
LANES = 128
HALF = 64

MESH = pl.DeviceIdType.MESH
HIGH = lax.Precision.HIGHEST
BF = jnp.bfloat16
F32 = jnp.float32


def mm(left, right):
    return lax.dot_general(left, right, (((1,), (0,)), ((), ())), preferred_element_type=F32)


def mm_nt(left, right, precision=None):
    return lax.dot_general(
        left, right, (((1,), (1,)), ((), ())), precision=precision, preferred_element_type=F32
    )


def mm_tn(left, right, precision=None):
    return lax.dot_general(
        left, right, (((0,), (0,)), ((), ())), precision=precision, preferred_element_type=F32
    )


def tables(tiles, bands, height, width):
    cols = np.zeros((tiles, width, 2 * LANES), np.float32)
    for t in range(tiles):
        for w in range(width):
            q = w + 3
            cols[t, w, (q % 2) * LANES + t * HALF + q // 2] = 1
    edge = np.zeros((tiles, 32, width), np.float32)
    halo = np.zeros((2, 16, 2 * LANES), np.float32)
    for t in range(tiles):
        for k in range(3):
            edge[t, t * 8 + k, width - 3 + k] = 1
            edge[t, 16 + t * 8 + k, k] = 1
            halo[0, t * 8 + k, (k % 2) * LANES + t * HALF + k // 2] = 1
            q = width + 3 + k
            halo[1, t * 8 + k, (q % 2) * LANES + t * HALF + q // 2] = 1
    rows = np.zeros((16, 16, 2, bands, 16), np.float32)
    for r in range(16):
        for c in range(bands):
            if r < 3:
                rows[r, c, 0, c, 13 + r] = 1
            else:
                rows[r, c, 1, c, r - 3] = 1
    rows = rows.reshape(256, 2 * bands * 16)
    taps = np.zeros((4, bands, 7, 8, 8, 2, 16), np.float32)
    for b in range(4):
        for c in range(bands):
            for u in range(7):
                for pc in range(2):
                    if 2 * b + pc < 7:
                        taps[b, c, u, 2 * b + pc, u, pc, c] = 1
    taps = taps.reshape(4, bands * 56, 256)
    return [jnp.asarray(x, BF) for x in (cols, edge, halo, rows, taps)]


def kernel(
    sizes,
    pix, w_taps, w_head, grid_t, neg, key_date, cols, edge, halo, rows, taps, place,
    loss_out, stem_out, head_out,
    pack, strips, blocks, image, w_all, gids, neg_t, count_t, member, hidden,
    keys, grads, g_acc, part, gather1, gather2, gather3,
    s_col, r_col, s_row, r_row, s_key, r_key, s_gra, r_gra, s_1, r_1, s_2, r_2, s_3, r_3,
):
    tiles, bands, height, width, n_row, n_col, dates = sizes
    fr, fc = height // 2, width // 2
    cells = fr // CELL * (fc // CELL)
    anchors = tiles * cells
    n_mem = n_row * n_col
    row, col, date = lax.axis_index("row"), lax.axis_index("col"), lax.axis_index("date")
    me = row * n_col + col

    barrier = pltpu.get_barrier_semaphore()
    members, peers = [], []
    for k in range(1, n_mem):
        other = lax.rem(me + k, n_mem)
        members.append((other, {"row": other // n_col, "col": lax.rem(other, n_col)}))
    for k in range(1, dates):
        other = lax.rem(date + k, dates)
        peers.append((other, {"date": other}))
    for _, dev in members + peers:
        pl.semaphore_signal(barrier, inc=1, device_id=dev, device_id_type=MESH)

    def pack_band(c, carry):
        both = mm_nt(edge[0], pix[0, c])
        for t in range(1, tiles):
            both += mm_nt(edge[t], pix[t, c])
        both = both.astype(BF)
        pack[0, c] = both[:16]
        pack[1, c] = both[16:]
        return carry

    lax.fori_loop(0, bands, pack_band, 0)
    pl.semaphore_wait(barrier, len(members) + len(peers))

    def copy(src, dst, send, recv, dev):
        return pltpu.make_async_remote_copy(
            src_ref=src, dst_ref=dst, send_sem=send, recv_sem=recv,
            device_id=dev, device_id_type=MESH,
        )

    to_right = copy(pack.at[0], strips.at[0], s_col.at[0], r_col.at[0], {"col": lax.rem(col + 1, n_col)})
    to_left = copy(pack.at[1], strips.at[1], s_col.at[1], r_col.at[1], {"col": lax.rem(col + n_col - 1, n_col)})
    down = copy(blocks.at[height // 16], blocks.at[0], s_row.at[0], r_row.at[0], {"row": lax.rem(row + 1, n_row)})
    up = copy(blocks.at[1], blocks.at[height // 16 + 1], s_row.at[1], r_row.at[1], {"row": lax.rem(row + n_row - 1, n_row)})

    @pl.when(col < n_col - 1)
    def _():
        to_right.start()

    @pl.when(col > 0)
    def _():
        to_left.start()

    @pl.when(col == 0)
    def _():
        strips[0] = jnp.zeros(strips.shape[1:], BF)

    @pl.when(col == n_col - 1)
    def _():
        strips[1] = jnp.zeros(strips.shape[1:], BF)

    for b in range(4):
        w_all[64 * b : 64 * b + 64, :] = mm_tn(w_taps[...], taps[b]).astype(BF)
    lane = lax.broadcasted_iota(jnp.int32, (1, LANES), 1)
    inside = lax.rem(lane, HALF) < fc
    shift = jnp.where(inside, (lane // HALF) * cells, -1000).astype(F32)
    gids[...] = mm_tn(grid_t[...].astype(F32).astype(BF), place[...]) + shift
    sub = lax.broadcasted_iota(jnp.int32, (anchors, 1), 0)
    key_ids = (lax.rem(sub, tiles) * cells + sub // tiles).astype(F32)
    eye_n = (
        lax.broadcasted_iota(jnp.int32, (neg.shape[1],) * 2, 0)
        == lax.broadcasted_iota(jnp.int32, (neg.shape[1],) * 2, 1)
    ).astype(F32).astype(BF)
    neg_t[...] = mm_nt(eye_n, neg[...].astype(F32).astype(BF))

    def count_step(s, total):
        for k in range(8):
            total += jnp.where(neg_t[pl.ds(s * 8 + k, 1), :] == key_ids, 1.0, 0.0)
        return total

    count_t[...] = lax.fori_loop(
        0, neg.shape[1] // 8, count_step, jnp.zeros((anchors, anchors), F32)
    )

    @pl.when(col > 0)
    def _():
        copy(pack.at[0], strips.at[0], s_col.at[0], r_col.at[0], {"col": lax.rem(col + n_col - 1, n_col)}).wait_recv()

    @pl.when(col < n_col - 1)
    def _():
        copy(pack.at[1], strips.at[1], s_col.at[1], r_col.at[1], {"col": lax.rem(col + 1, n_col)}).wait_recv()

    def own_band(c, carry):
        wide = mm_tn(strips[0, c], halo[0]) + mm_tn(strips[1, c], halo[1])
        for t in range(tiles):
            wide += mm(pix[t, c], cols[t])
        blocks[pl.ds(1, height // 16), c] = wide.astype(BF).reshape(height // 16, 16, 2 * LANES)
        return carry

    lax.fori_loop(0, bands, own_band, 0)

    @pl.when(row < n_row - 1)
    def _():
        down.start()

    @pl.when(row > 0)
    def _():
        up.start()

    @pl.when(row == 0)
    def _():
        blocks[0] = jnp.zeros(blocks.shape[1:], BF)

    @pl.when(row == n_row - 1)
    def _():
        blocks[height // 16 + 1] = jnp.zeros(blocks.shape[1:], BF)

    @pl.when(row > 0)
    def _():
        copy(blocks.at[height // 16], blocks.at[0], s_row.at[0], r_row.at[0], {"row": lax.rem(row + n_row - 1, n_row)}).wait_recv()

    @pl.when(row < n_row - 1)
    def _():
        copy(blocks.at[1], blocks.at[height // 16 + 1], s_row.at[1], r_row.at[1], {"row": lax.rem(row + 1, n_row)}).wait_recv()

    def image_step(k, carry):
        pair = blocks[pl.ds(k, 2)].reshape(2 * bands * 16, 2 * LANES)
        out = mm(rows[...], pair).astype(BF)
        for pc in range(2):
            image[pl.ds(k * 8, 8), :, pc] = out[:, pc * LANES : (pc + 1) * LANES].reshape(8, 2, 16, LANES)
        return carry

    lax.fori_loop(0, height // 16 + 1, image_step, 0)

    def wide_rows(s):
        return jnp.concatenate(
            [image[pl.ds(s * STEP + r, 4)].reshape(256, LANES) for r in range(STEP)], axis=1
        )

    def forward_step(s, total):
        taps_out = mm(w_all[...], wide_rows(s))
        hid, mem = [], []
        for r in range(STEP):
            part_r = taps_out[:, r * LANES : (r + 1) * LANES]
            stem = part_r[:64]
            for b in range(1, 4):
                stem += pltpu.roll(part_r[64 * b : 64 * b + 64], LANES - b, 1)
            hid.append(jnp.maximum(stem, 0.0).astype(BF))
            mem.append(jnp.where(gids[pl.ds(s * STEP + r, 1), :] == key_ids, 1.0, 0.0).astype(BF))
        hid = jnp.concatenate(hid, axis=1)
        mem = jnp.concatenate(mem, axis=1)
        hidden[s] = hid
        member[s] = mem
        return total + mm_nt(mem, jnp.concatenate([hid, jnp.ones_like(hid)], axis=0))

    sums = lax.fori_loop(0, fr // STEP, forward_step, jnp.zeros((anchors, LANES), F32))
    counts = sums[:, 64:]
    pooled = sums[:, :64] / counts
    head = w_head[...]
    project = lax.dot_general(
        pooled, head, (((1,), (0,)), ((), ())), precision=HIGH, preferred_element_type=F32
    )
    length = jnp.sqrt(jnp.sum(project * project, axis=1, keepdims=True) + EPS)
    embed = project / length
    keys[pl.ds(date, 1)] = embed[None]
    sends = [copy(keys.at[date], keys.at[date], s_key.at[o], r_key.at[date], dev) for o, dev in peers]
    for c in sends:
        c.start()
    for o, dev in peers:
        copy(keys.at[o], keys.at[o], s_key.at[o], r_key.at[o], dev).wait_recv()
    target = key_date[date]
    key_rows = keys[target]
    scores = mm_nt(key_rows, embed, HIGH) / TEMP
    same = lax.broadcasted_iota(jnp.int32, (anchors, anchors), 0) == lax.broadcasted_iota(
        jnp.int32, (anchors, anchors), 1
    )
    positive = jnp.sum(jnp.where(same, scores, 0.0), axis=0, keepdims=True)
    weights = count_t[...] * jnp.exp(scores)
    exp_pos = jnp.exp(positive)
    denominator = exp_pos + jnp.sum(weights, axis=0, keepdims=True)
    loss_out[...] = jnp.log(denominator) - positive
    scale = 1.0 / math.sqrt(dates * anchors * n_mem)
    d_scores = (scale / TEMP) * (
        weights / denominator + jnp.where(same, exp_pos / denominator - 1.0, 0.0)
    )
    grads[pl.ds(date, 1)] = lax.dot_general(
        d_scores, embed, (((1,), (0,)), ((), ())), precision=HIGH, preferred_element_type=F32
    )[None]
    more = [copy(grads.at[date], grads.at[date], s_gra.at[o], r_gra.at[date], dev) for o, dev in peers]
    for c in more:
        c.start()
    grad_anchor = mm_tn(d_scores, key_rows, HIGH)
    for o, dev in peers:
        copy(grads.at[o], grads.at[o], s_gra.at[o], r_gra.at[o], dev).wait_recv()
    returned = jnp.zeros_like(grad_anchor)
    for d in range(dates):
        returned += jnp.where(key_date[d] == date, grads[d], 0.0)
    grad_embed = grad_anchor + returned
    grad_project = (
        grad_embed - embed * jnp.sum(embed * grad_embed, axis=1, keepdims=True)
    ) / length
    head_term = mm_tn(pooled, grad_project, HIGH)
    per_cell = (mm_nt(grad_project, head, HIGH) / counts).astype(BF)
    eye_c = (
        lax.broadcasted_iota(jnp.int32, (64, 64), 0) == lax.broadcasted_iota(jnp.int32, (64, 64), 1)
    ).astype(F32).astype(BF)
    cell_t = mm_nt(eye_c, per_cell).astype(BF)

    g_acc[...] = jnp.zeros_like(g_acc)

    def backward_step(s, carry):
        spread = mm(cell_t, member[s])
        slope = jnp.where(hidden[s].astype(F32) > 0.0, spread, 0.0)
        moved = [slope.astype(BF)]
        for b in range(1, 4):
            moved.append(
                jnp.concatenate(
                    [pltpu.roll(slope[:, r * LANES : (r + 1) * LANES], b, 1) for r in range(STEP)],
                    axis=1,
                ).astype(BF)
            )
        g_acc[...] += mm_nt(jnp.concatenate(moved, axis=0), wide_rows(s))
        return carry

    lax.fori_loop(0, fr // STEP, backward_step, 0)

    gr, hr = 256 // n_mem, 64 // n_mem
    for m in range(n_mem):
        part[m, :gr] = g_acc[m * gr : (m + 1) * gr]
        part[m, gr:] = jnp.concatenate([head_term[m * hr : (m + 1) * hr]] * 2, axis=1)
    sends += more
    gather1[pl.ds(me, 1)] = part[pl.ds(me, 1)]
    step1 = [copy(part.at[o], gather1.at[me], s_1.at[o], r_1.at[me], dev) for o, dev in members]
    for c in step1:
        c.start()
    for o, dev in members:
        copy(part.at[o], gather1.at[o], s_1.at[o], r_1.at[o], dev).wait_recv()
    total = gather1[0]
    for m in range(1, n_mem):
        total += gather1[m]
    gather2[pl.ds(date, 1)] = total[None]
    step2 = [copy(gather2.at[date], gather2.at[date], s_2.at[o], r_2.at[date], dev) for o, dev in peers]
    for c in step2:
        c.start()
    for o, dev in peers:
        copy(gather2.at[o], gather2.at[o], s_2.at[o], r_2.at[o], dev).wait_recv()
    total = gather2[0]
    for d in range(1, dates):
        total += gather2[d]
    gather3[pl.ds(me, 1)] = total[None]
    step3 = [copy(gather3.at[me], gather3.at[me], s_3.at[o], r_3.at[me], dev) for o, dev in members]
    for c in step3:
        c.start()
    for o, dev in members:
        copy(gather3.at[o], gather3.at[o], s_3.at[o], r_3.at[o], dev).wait_recv()
    for m in range(n_mem):
        head_out[m * hr : (m + 1) * hr] = gather3[m, gr:, :LANES]
        g_acc[m * gr : (m + 1) * gr] = gather3[m, :gr]
    result = jnp.zeros((bands * 56, 64), F32)
    for b in range(4):
        whole = g_acc[64 * b : 64 * b + 64]
        high = whole.astype(BF)
        rest = whole - high.astype(F32)
        mid = rest.astype(BF)
        low = (rest - mid.astype(F32)).astype(BF)
        result += mm_nt(taps[b], high) + (mm_nt(taps[b], mid) + mm_nt(taps[b], low))
    stem_out[...] = result.reshape(bands, 7, 8, 64)[:, :, :7, :]

    for c in sends + step1 + step2 + step3:
        c.wait_send()

    @pl.when(col < n_col - 1)
    def _():
        to_right.wait_send()

    @pl.when(col > 0)
    def _():
        to_left.wait_send()

    @pl.when(row < n_row - 1)
    def _():
        down.wait_send()

    @pl.when(row > 0)
    def _():
        up.wait_send()


def solution(mesh):
    n_row, n_col, dates = mesh.shape["row"], mesh.shape["col"], mesh.shape["date"]

    def local(pixels, w_stem, w_head, pool_grid, neg_index, key_date):
        _, tiles, bands, height, width = pixels.shape
        fr, fc = height // 2, width // 2
        cells = fr // CELL * (fc // CELL)
        anchors = tiles * cells
        n_mem = n_row * n_col
        chunk = (256 + 64) // n_mem
        w_taps = jnp.pad(jnp.transpose(w_stem, (1, 2, 3, 0)), ((0, 0), (0, 0), (0, 1), (0, 0)))
        w_taps = w_taps.reshape(bands * 56, 64)
        grid_t = pool_grid.T
        neg = jnp.transpose(neg_index[0], (1, 2, 0, 3)).reshape(anchors, -1)
        place = np.zeros((fc, LANES), np.float32)
        for j in range(fc):
            for t in range(tiles):
                place[j, t * HALF + j] = 1
        vmem = pl.BlockSpec(memory_space=pltpu.VMEM)
        dma = pltpu.SemaphoreType.DMA
        loss, stem, head = pl.pallas_call(
            functools.partial(kernel, (tiles, bands, height, width, n_row, n_col, dates)),
            out_shape=(
                jax.ShapeDtypeStruct((1, anchors), F32),
                jax.ShapeDtypeStruct((bands, 7, 7, 64), F32),
                jax.ShapeDtypeStruct((64, LANES), F32),
            ),
            in_specs=[vmem] * 5 + [pl.BlockSpec(memory_space=pltpu.SMEM)] + [vmem] * 6,
            out_specs=(vmem, vmem, vmem),
            scratch_shapes=[
                pltpu.VMEM((2, bands, 16, height), BF),
                pltpu.VMEM((2, bands, 16, height), BF),
                pltpu.VMEM((height // 16 + 2, bands, 16, 2 * LANES), BF),
                pltpu.VMEM((height // 2 + 8, 2, 2, 16, LANES), BF),
                pltpu.VMEM((256, 256), BF),
                pltpu.VMEM((fr, LANES), F32),
                pltpu.VMEM((neg.shape[1], anchors), F32),
                pltpu.VMEM((anchors, anchors), F32),
                pltpu.VMEM((fr // STEP, anchors, STEP * LANES), BF),
                pltpu.VMEM((fr // STEP, 64, STEP * LANES), BF),
                pltpu.VMEM((dates, anchors, LANES), F32),
                pltpu.VMEM((dates, anchors, LANES), F32),
                pltpu.VMEM((256, 256), F32),
                pltpu.VMEM((n_mem, chunk, 256), F32),
                pltpu.VMEM((n_mem, chunk, 256), F32),
                pltpu.VMEM((dates, chunk, 256), F32),
                pltpu.VMEM((n_mem, chunk, 256), F32),
                dma((2,)), dma((2,)), dma((2,)), dma((2,)),
                dma((dates,)), dma((dates,)), dma((dates,)), dma((dates,)),
                dma((n_mem,)), dma((n_mem,)), dma((dates,)), dma((dates,)),
                dma((n_mem,)), dma((n_mem,)),
            ],
            compiler_params=pltpu.CompilerParams(
                collective_id=0, has_side_effects=True, vmem_limit_bytes=48 * 2**20
            ),
        )(
            pixels[0], w_taps, w_head, grid_t, neg, key_date,
            *tables(tiles, bands, height, width), jnp.asarray(place, BF),
        )
        loss = loss.reshape(fr // CELL, fc // CELL, tiles).transpose(2, 0, 1)[None]
        return loss, jnp.transpose(stem, (3, 0, 1, 2)), head

    return jax.shard_map(
        local,
        mesh=mesh,
        in_specs=(
            P(("groups", "date"), None, None, "row", "col"),
            P(),
            P(),
            P("row", "col"),
            P(("groups", "date"), None, "row", "col", None),
            P(),
        ),
        out_specs=(
            P(("groups", "date"), None, "row", "col"),
            P("groups", None, None, None),
            P("groups", None),
        ),
        check_vma=False,
    )
```

time: 799 us -> 92.2 us (0.12)
  local copies, waits for them, and re-layouts: 258 us -> 13.4 us
  other arithmetic: 230 us -> 0.66 us
  matrix products: 153 us -> 0 us
  blocking collectives: 87.2 us -> 0 us
  Pallas kernels: 0 us -> 76.9 us
  waiting for transfers between devices: 36.2 us -> 0 us
  between operations: 18.9 us -> 0.67 us
  starting transfers between devices: 9.44 us -> 0 us
    gather x7 -> x0, local copies, waits for them, and re-layouts: 167 us -> none  [the longest x3 146 us: local(): negative = jnp.take_along_axis(scores, neg_rows, axis=1)]
    transpose x1 -> x0, matrix products: 131 us -> none  [weight_term(): return jnp.transpose(result, (1, 0, 2, 3))]
    unnamed x4 -> x0, other arithmetic: 126 us -> none
    pallas_call x0 -> x1, Pallas kernels: none -> 76.9 us  [local(): pl.pallas_call(functools.partial(kernel, (tiles, bands, height, width, n_...]
    psum x1 -> x0, blocking collectives: 58.3 us -> none  [local(): lax.psum((stem_term, head_term), ('date', 'row', 'col'))]
    concatenate x3 -> x0, other arithmetic: 42.7 us -> none  [the longest x1 42.7 us: padded_2(): array = jnp.concatenate([before, array, after], axis=dim)]
    transpose x2 -> x0, other arithmetic: 41.4 us -> none  [the longest x1 41.4 us: weight_term(): return jnp.transpose(result, (1, 0, 2, 3))]
    psum x1 -> x0, waiting for transfers between devices: 30.4 us -> none  [local(): lax.psum((stem_term, head_term), ('date', 'row', 'col'))]
  transfers between devices with their start and end apart: 5 -> 0, of which waited for: 3 -> 0; matrix products, arithmetic and copies ran while one was open for 1% -> 0% of each run, Pallas kernels for 0% -> 0%
where the time goes in v1:
time: 92.2 us; the launch traced here: 91.6 us
  Pallas kernels  76.9 us (83%)
  local copies, waits for them, and re-layouts  13.4 us (15%)
    pallas_call x1, Pallas kernels, local(): pl.pallas_call(functools.partial(kernel, (tiles, bands, height, width, n_...  76.9 us
    unnamed x25, local copies, waits for them, and re-layouts  11.8 us

profile of v1, /device:TPU:0, one launch (start us, length us, event | category | flops | bytes accessed | tf_op | source)
XLA Modules:
  0.0 91.6 jit_solution(7909190557075286449)
XLA Ops:
  0.6 1.0 %pad.4 = bf16[13,7,8,64]{3,2,1,0:T(8,128)(2,1)S(1)} pad(bf16[13,7,7,64]{3,2,1,0:T(8,128)(2,1)} %bitcast.19, bf16[]{:T(256)} %constant.14.clone.1), padding=0_0x0_0x0_1x0_0 | pad | bytes 174722 | tf_op jit(solution)/shard_map/jit(_pad)/pad | solution.py:378
  1.6 0.0 copy-start
  1.6 1.4 %copy-done = bf16[4,728,256]{2,1,0:T(8,128)(2,1)S(1)} copy-done((bf16[4,728,256]{2,1,0:T(8,128)(2,1)S(1)}, bf16[4,728,256]{2,1,0:T(8,128)(2,1)}, u32[]{:S(2)}) %copy-start) | copy-done | bytes 1490968
  3.0 0.0 copy-start.1
  3.0 1.3 %copy-done.1 = bf16[1,2,13,192,96]{4,3,2,1,0:T(8,128)(2,1)S(1)} copy-done((bf16[1,2,13,192,96]{4,3,2,1,0:T(8,128)(2,1)S(1)}, bf16[1,2,13,192,96]{4,3,2,1,0:T(8,128)(2,1)}, u32[]{:S(2)}) %copy-start.1) | copy-done | bytes 958488
  4.3 0.0 copy-start.2
  4.3 0.9 %copy-done.2 = bf16[256,416]{1,0:T(8,128)(2,1)S(1)} copy-done((bf16[256,416]{1,0:T(8,128)(2,1)S(1)}, bf16[256,416]{1,0:T(8,128)(2,1)}, u32[]{:S(2)}) %copy-start.2) | copy-done | bytes 213016
  5.2 0.0 copy-start.3
  5.3 0.9 copy-done.3
  6.1 0.0 copy-start.4
  6.1 0.9 copy-done.4
  7.0 0.0 copy-start.5
  7.0 0.8 copy-done.5
  7.8 0.0 copy-start.6
  7.8 0.7 copy-done.6
  8.5 0.0 copy-start.7
  8.5 0.7 copy-done.7
  9.2 0.0 copy-start.8
  9.2 0.7 copy-done.8
  10.0 0.0 copy-start.9
  10.0 0.7 copy-done.9
  10.7 0.0 copy-start.10
  10.7 0.7 copy-done.10
  11.3 76.9 %shard_map.139 = (f32[1,144]{1,0:T(1,128)S(1)}, f32[13,7,7,64]{3,2,1,0:T(8,128)S(1)}, f32[64,128]{1,0:T(8,128)S(1)}) custom-call(bf16[2,13,192,96]{3,2,1,0:T(8,128)(2,1)S(1)} %bitcast.13, bf16[728,64]{1,0:T(8,128)(2,1)S(1)} %bitcast.14, f32[64,128]{1,0:T(8,128)S(1)} %copy-done.5, s32[48,96]{1,0:T(8,128)S(1)} %bitcast.17, s32[144,128]{1,0:T(8,128)S(1)} %bitcast.16, ...), custom_call_target="tpu_custom_call" | custom-call | tf_op jit(solution)/shard_map/pallas_call | solution.py:388
  88.2 0.5 broadcast.5
  88.7 0.7 reduce.3
  89.4 0.1 reshape.17
  89.5 0.7 copy.16
  90.2 0.7 copy.19
  91.0 0.6 copy.20
Async XLA Ops:
  1.6 1.4 %copy-start = (bf16[4,728,256]{2,1,0:T(8,128)(2,1)S(1)}, bf16[4,728,256]{2,1,0:T(8,128)(2,1)}, u32[]{:S(2)}) copy-start(bf16[4,728,256]{2,1,0:T(8,128)(2,1)} %constant.19.clone.taps) | copy-start | bytes 4472836
  3.0 1.3 %copy-start.1 = (bf16[1,2,13,192,96]{4,3,2,1,0:T(8,128)(2,1)S(1)}, bf16[1,2,13,192,96]{4,3,2,1,0:T(8,128)(2,1)}, u32[]{:S(2)}) copy-start(bf16[1,2,13,192,96]{4,3,2,1,0:T(8,128)(2,1)} %param.12) | copy-start | bytes 2875396
  4.3 0.9 %copy-start.2 = (bf16[256,416]{1,0:T(8,128)(2,1)S(1)}, bf16[256,416]{1,0:T(8,128)(2,1)}, u32[]{:S(2)}) copy-start(bf16[256,416]{1,0:T(8,128)(2,1)} %constant.18.clone.rows) | copy-start | bytes 638980
  5.2 0.9 copy-start.3
  6.1 0.9 copy-start.4
  7.0 0.8 copy-start.5
  7.8 0.7 copy-start.6
  8.5 0.7 copy-start.7
  9.2 0.7 copy-start.8
  10.0 0.7 copy-start.9
  10.7 0.7 copy-start.10

commit v2 on v1

--- a/solution.py
+++ b/solution.py
@@ -24,6 +24,22 @@
 
 def mm(left, right):
     return lax.dot_general(left, right, (((1,), (0,)), ((), ())), preferred_element_type=F32)
+
+
+def mm_high(left, right):
+    return lax.dot_general(
+        left, right, (((1,), (0,)), ((), ())), precision=HIGH, preferred_element_type=F32
+    )
+
+
+def fold(array):
+    half = array.shape[0] // 2
+    return jnp.concatenate([array[:half], array[half:]], axis=1)
+
+
+def unfold(array):
+    half = array.shape[1] // 2
+    return jnp.concatenate([array[:, :half], array[:, half:]], axis=0)
 
 
 def mm_nt(left, right, precision=None):
@@ -74,11 +90,22 @@
 
 def kernel(
     sizes,
-    pix, w_taps, w_head, grid_t, neg, key_date, cols, edge, halo, rows, taps, place,
-    loss_out, stem_out, head_out,
+    *refs,
+):
+    n_in = 12
+    sources, (loss_out, stem_out, head_out) = refs[:n_in], refs[n_in : n_in + 3]
+    held, rest = refs[n_in + 3 : 2 * n_in + 3], refs[2 * n_in + 3 :]
+    pix, edge, w_taps, taps, grid_t, place, neg, cols, halo, rows, w_head, key_date = held
+    body(sizes, sources, held, loss_out, stem_out, head_out,
+         pix, edge, w_taps, taps, grid_t, place, neg, cols, halo, rows, w_head, key_date, *rest)
+
+
+def body(
+    sizes, sources, held, loss_out, stem_out, head_out,
+    pix, edge, w_taps, taps, grid_t, place, neg, cols, halo, rows, w_head, key_date,
     pack, strips, blocks, image, w_all, gids, neg_t, count_t, member, hidden,
     keys, grads, g_acc, part, gather1, gather2, gather3,
-    s_col, r_col, s_row, r_row, s_key, r_key, s_gra, r_gra, s_1, r_1, s_2, r_2, s_3, r_3,
+    s_col, r_col, s_row, r_row, s_key, r_key, s_gra, r_gra, s_1, r_1, s_2, r_2, s_3, r_3, s_in,
 ):
     tiles, bands, height, width, n_row, n_col, dates = sizes
     fr, fc = height // 2, width // 2
@@ -88,6 +115,9 @@
     row, col, date = lax.axis_index("row"), lax.axis_index("col"), lax.axis_index("date")
     me = row * n_col + col
 
+    fetches = [pltpu.make_async_copy(a, b, s_in.at[i]) for i, (a, b) in enumerate(zip(sources, held))]
+    for c in fetches:
+        c.start()
     barrier = pltpu.get_barrier_semaphore()
     members, peers = [], []
     for k in range(1, n_mem):
@@ -99,6 +129,9 @@
     for _, dev in members + peers:
         pl.semaphore_signal(barrier, inc=1, device_id=dev, device_id_type=MESH)
 
+    fetches[0].wait()
+    fetches[1].wait()
+
     def pack_band(c, carry):
         both = mm_nt(edge[0], pix[0, c])
         for t in range(1, tiles):
@@ -108,7 +141,7 @@
         pack[1, c] = both[16:]
         return carry
 
-    lax.fori_loop(0, bands, pack_band, 0)
+    lax.fori_loop(0, bands, pack_band, 0, unroll=True)
     pl.semaphore_wait(barrier, len(members) + len(peers))
 
     def copy(src, dst, send, recv, dev):
@@ -138,6 +171,8 @@
     def _():
         strips[1] = jnp.zeros(strips.shape[1:], BF)
 
+    for c in fetches[2:]:
+        c.wait()
     for b in range(4):
         w_all[64 * b : 64 * b + 64, :] = mm_tn(w_taps[...], taps[b]).astype(BF)
     lane = lax.broadcasted_iota(jnp.int32, (1, LANES), 1)
@@ -176,7 +211,7 @@
         blocks[pl.ds(1, height // 16), c] = wide.astype(BF).reshape(height // 16, 16, 2 * LANES)
         return carry
 
-    lax.fori_loop(0, bands, own_band, 0)
+    lax.fori_loop(0, bands, own_band, 0, unroll=True)
 
     @pl.when(row < n_row - 1)
     def _():
@@ -209,7 +244,7 @@
             image[pl.ds(k * 8, 8), :, pc] = out[:, pc * LANES : (pc + 1) * LANES].reshape(8, 2, 16, LANES)
         return carry
 
-    lax.fori_loop(0, height // 16 + 1, image_step, 0)
+    lax.fori_loop(0, height // 16 + 1, image_step, 0, unroll=True)
 
     def wide_rows(s):
         return jnp.concatenate(
@@ -236,20 +271,20 @@
     counts = sums[:, 64:]
     pooled = sums[:, :64] / counts
     head = w_head[...]
-    project = lax.dot_general(
-        pooled, head, (((1,), (0,)), ((), ())), precision=HIGH, preferred_element_type=F32
-    )
+    project = mm_high(pooled, head)
     length = jnp.sqrt(jnp.sum(project * project, axis=1, keepdims=True) + EPS)
     embed = project / length
-    keys[pl.ds(date, 1)] = embed[None]
+    short = pooled / length
+    keys[pl.ds(date, 1)] = fold(short)[None]
     sends = [copy(keys.at[date], keys.at[date], s_key.at[o], r_key.at[date], dev) for o, dev in peers]
     for c in sends:
         c.start()
+    back = mm_nt(embed, head, HIGH)
     for o, dev in peers:
         copy(keys.at[o], keys.at[o], s_key.at[o], r_key.at[o], dev).wait_recv()
     target = key_date[date]
-    key_rows = keys[target]
-    scores = mm_nt(key_rows, embed, HIGH) / TEMP
+    key_short = unfold(keys[target])
+    scores = mm_nt(key_short, back, HIGH) / TEMP
     same = lax.broadcasted_iota(jnp.int32, (anchors, anchors), 0) == lax.broadcasted_iota(
         jnp.int32, (anchors, anchors), 1
     )
@@ -257,24 +292,29 @@
     weights = count_t[...] * jnp.exp(scores)
     exp_pos = jnp.exp(positive)
     denominator = exp_pos + jnp.sum(weights, axis=0, keepdims=True)
-    loss_out[...] = jnp.log(denominator) - positive
     scale = 1.0 / math.sqrt(dates * anchors * n_mem)
     d_scores = (scale / TEMP) * (
         weights / denominator + jnp.where(same, exp_pos / denominator - 1.0, 0.0)
     )
-    grads[pl.ds(date, 1)] = lax.dot_general(
-        d_scores, embed, (((1,), (0,)), ((), ())), precision=HIGH, preferred_element_type=F32
-    )[None]
+    grads[pl.ds(date, 1)] = fold(mm_high(d_scores, short))[None]
     more = [copy(grads.at[date], grads.at[date], s_gra.at[o], r_gra.at[date], dev) for o, dev in peers]
     for c in more:
         c.start()
-    grad_anchor = mm_tn(d_scores, key_rows, HIGH)
+    grad_short = mm_tn(d_scores, key_short, HIGH)
+    losses = jnp.log(denominator) - positive
+    n_down, n_across = fr // CELL, fc // CELL
+    wide = n_across * tiles
+    spot = lax.broadcasted_iota(jnp.int32, (wide, anchors), 1)
+    pick = jnp.where(lax.rem(spot, wide) == lax.broadcasted_iota(jnp.int32, (wide, anchors), 0), losses, 0.0)
+    line = lax.broadcasted_iota(jnp.int32, (n_down, anchors), 1) // wide
+    lines = (line == lax.broadcasted_iota(jnp.int32, (n_down, anchors), 0)).astype(F32)
+    loss_out[...] = mm_nt(pick, lines, HIGH).reshape(n_across, tiles, n_down)
     for o, dev in peers:
         copy(grads.at[o], grads.at[o], s_gra.at[o], r_gra.at[o], dev).wait_recv()
-    returned = jnp.zeros_like(grad_anchor)
+    returned = jnp.zeros(grads.shape[1:], F32)
     for d in range(dates):
         returned += jnp.where(key_date[d] == date, grads[d], 0.0)
-    grad_embed = grad_anchor + returned
+    grad_embed = mm_high(grad_short + unfold(returned), head)
     grad_project = (
         grad_embed - embed * jnp.sum(embed * grad_embed, axis=1, keepdims=True)
     ) / length
@@ -305,8 +345,8 @@
 
     gr, hr = 256 // n_mem, 64 // n_mem
     for m in range(n_mem):
-        part[m, :gr] = g_acc[m * gr : (m + 1) * gr]
-        part[m, gr:] = jnp.concatenate([head_term[m * hr : (m + 1) * hr]] * 2, axis=1)
+        part[m, :gr] = g_acc[m * gr : (m + 1) * gr].astype(BF)
+        part[m, gr:] = jnp.concatenate([head_term[m * hr : (m + 1) * hr]] * 2, axis=1).astype(BF)
     sends += more
     gather1[pl.ds(me, 1)] = part[pl.ds(me, 1)]
     step1 = [copy(part.at[o], gather1.at[me], s_1.at[o], r_1.at[me], dev) for o, dev in members]
@@ -314,35 +354,30 @@
         c.start()
     for o, dev in members:
         copy(part.at[o], gather1.at[o], s_1.at[o], r_1.at[o], dev).wait_recv()
-    total = gather1[0]
+    total = gather1[0].astype(F32)
     for m in range(1, n_mem):
-        total += gather1[m]
-    gather2[pl.ds(date, 1)] = total[None]
+        total += gather1[m].astype(F32)
+    gather2[pl.ds(date, 1)] = total.astype(BF)[None]
     step2 = [copy(gather2.at[date], gather2.at[date], s_2.at[o], r_2.at[date], dev) for o, dev in peers]
     for c in step2:
         c.start()
     for o, dev in peers:
         copy(gather2.at[o], gather2.at[o], s_2.at[o], r_2.at[o], dev).wait_recv()
-    total = gather2[0]
+    total = gather2[0].astype(F32)
     for d in range(1, dates):
-        total += gather2[d]
-    gather3[pl.ds(me, 1)] = total[None]
+        total += gather2[d].astype(F32)
+    gather3[pl.ds(me, 1)] = total.astype(BF)[None]
     step3 = [copy(gather3.at[me], gather3.at[me], s_3.at[o], r_3.at[me], dev) for o, dev in members]
     for c in step3:
         c.start()
     for o, dev in members:
         copy(gather3.at[o], gather3.at[o], s_3.at[o], r_3.at[o], dev).wait_recv()
     for m in range(n_mem):
-        head_out[m * hr : (m + 1) * hr] = gather3[m, gr:, :LANES]
-        g_acc[m * gr : (m + 1) * gr] = gather3[m, :gr]
+        head_out[m * hr : (m + 1) * hr] = gather3[m, gr:, :LANES].astype(F32)
     result = jnp.zeros((bands * 56, 64), F32)
+    whole = jnp.concatenate([gather3[m, :gr] for m in range(n_mem)], axis=0)
     for b in range(4):
-        whole = g_acc[64 * b : 64 * b + 64]
-        high = whole.astype(BF)
-        rest = whole - high.astype(F32)
-        mid = rest.astype(BF)
-        low = (rest - mid.astype(F32)).astype(BF)
-        result += mm_nt(taps[b], high) + (mm_nt(taps[b], mid) + mm_nt(taps[b], low))
+        result += mm_nt(taps[b], whole[64 * b : 64 * b + 64])
     stem_out[...] = result.reshape(bands, 7, 8, 64)[:, :, :7, :]
 
     for c in sends + step1 + step2 + step3:
@@ -385,16 +420,23 @@
                 place[j, t * HALF + j] = 1
         vmem = pl.BlockSpec(memory_space=pltpu.VMEM)
         dma = pltpu.SemaphoreType.DMA
+        cols, edge, halo, rows, taps = tables(tiles, bands, height, width)
+        operands = (
+            pixels[0], edge, w_taps, taps, grid_t, jnp.asarray(place, BF), neg, cols, halo, rows,
+            w_head, key_date,
+        )
         loss, stem, head = pl.pallas_call(
             functools.partial(kernel, (tiles, bands, height, width, n_row, n_col, dates)),
             out_shape=(
-                jax.ShapeDtypeStruct((1, anchors), F32),
+                jax.ShapeDtypeStruct((fc // CELL, tiles, fr // CELL), F32),
                 jax.ShapeDtypeStruct((bands, 7, 7, 64), F32),
                 jax.ShapeDtypeStruct((64, LANES), F32),
             ),
-            in_specs=[vmem] * 5 + [pl.BlockSpec(memory_space=pltpu.SMEM)] + [vmem] * 6,
+            in_specs=[pl.BlockSpec(memory_space=pltpu.HBM)] * len(operands),
             out_specs=(vmem, vmem, vmem),
-            scratch_shapes=[
+            scratch_shapes=[pltpu.VMEM(x.shape, x.dtype) for x in operands[:-1]]
+            + [pltpu.SMEM(key_date.shape, key_date.dtype)]
+            + [
                 pltpu.VMEM((2, bands, 16, height), BF),
                 pltpu.VMEM((2, bands, 16, height), BF),
                 pltpu.VMEM((height // 16 + 2, bands, 16, 2 * LANES), BF),
@@ -405,26 +447,23 @@
                 pltpu.VMEM((anchors, anchors), F32),
                 pltpu.VMEM((fr // STEP, anchors, STEP * LANES), BF),
                 pltpu.VMEM((fr // STEP, 64, STEP * LANES), BF),
-                pltpu.VMEM((dates, anchors, LANES), F32),
-                pltpu.VMEM((dates, anchors, LANES), F32),
+                pltpu.VMEM((dates, anchors // 2, LANES), F32),
+                pltpu.VMEM((dates, anchors // 2, LANES), F32),
                 pltpu.VMEM((256, 256), F32),
-                pltpu.VMEM((n_mem, chunk, 256), F32),
-                pltpu.VMEM((n_mem, chunk, 256), F32),
-                pltpu.VMEM((dates, chunk, 256), F32),
-                pltpu.VMEM((n_mem, chunk, 256), F32),
+                pltpu.VMEM((n_mem, chunk, 256), BF),
+                pltpu.VMEM((n_mem, chunk, 256), BF),
+                pltpu.VMEM((dates, chunk, 256), BF),
+                pltpu.VMEM((n_mem, chunk, 256), BF),
                 dma((2,)), dma((2,)), dma((2,)), dma((2,)),
                 dma((dates,)), dma((dates,)), dma((dates,)), dma((dates,)),
                 dma((n_mem,)), dma((n_mem,)), dma((dates,)), dma((dates,)),
-                dma((n_mem,)), dma((n_mem,)),
+                dma((n_mem,)), dma((n_mem,)), dma((len(operands),)),
             ],
             compiler_params=pltpu.CompilerParams(
-                collective_id=0, has_side_effects=True, vmem_limit_bytes=48 * 2**20
+                collective_id=0, has_side_effects=True, vmem_limit_bytes=60 * 2**20
             ),
-        )(
-            pixels[0], w_taps, w_head, grid_t, neg, key_date,
-            *tables(tiles, bands, height, width), jnp.asarray(place, BF),
-        )
-        loss = loss.reshape(fr // CELL, fc // CELL, tiles).transpose(2, 0, 1)[None]
+        )(*operands)
+        loss = loss.transpose(1, 2, 0)[None]
         return loss, jnp.transpose(stem, (3, 0, 1, 2)), head
 
     return jax.shard_map(

time: 92.2 us -> 67.9 us (0.74)
  Pallas kernels: 76.9 us -> 60.9 us
  local copies, waits for them, and re-layouts: 13.4 us -> 6.06 us
    pallas_call x1, Pallas kernels: 76.9 us -> 60.9 us  [local(): pl.pallas_call(functools.partial(kernel, (tiles, bands, height, width, n_...]
    unnamed x25 -> x3, local copies, waits for them, and re-layouts: 11.8 us -> 4.41 us
where the time goes in v2:
time: 67.9 us; the launch traced here: 67.6 us
  Pallas kernels  60.9 us (90%)
  local copies, waits for them, and re-layouts  6.06 us (9%)
    pallas_call x1, Pallas kernels, local(): pl.pallas_call(functools.partial(kernel, (tiles, bands, height, width, n_...  60.9 us
    unnamed x3, local copies, waits for them, and re-layouts  4.41 us
    pad x1, local copies, waits for them, and re-layouts, local(): jnp.pad(jnp.transpose(w_stem, (1, 2, 3, 0)), ((0, 0), (0, 0), (0, 1), (0,...  1.65 us

profile of v2, /device:TPU:0, one launch (start us, length us, event | category | flops | bytes accessed | tf_op | source)
XLA Modules:
  0.0 67.6 jit_solution(16265478904930698041)
XLA Ops:
  0.6 1.6 %pad.4 = bf16[13,7,8,64]{3,2,1,0:T(8,128)(2,1)} pad(bf16[13,7,7,64]{3,2,1,0:T(8,128)(2,1)} %bitcast.16, bf16[]{:T(256)} %constant.14.clone.1), padding=0_0x0_0x0_1x0_0 | pad | bytes 174722 | tf_op jit(solution)/shard_map/jit(_pad)/pad | solution.py:413
  2.3 60.9 %shard_map.139 = (f32[6,2,12]{2,1,0:T(2,128)}, f32[13,7,7,64]{3,2,1,0:T(8,128)}, f32[64,128]{1,0:T(8,128)}) custom-call(bf16[2,13,192,96]{3,2,1,0:T(8,128)(2,1)} %bitcast.13, bf16[2,32,96]{2,1,0:T(8,128)(2,1)} %constant.16.clone.refs_1_, bf16[728,64]{1,0:T(8,128)(2,1)} %bitcast.14, bf16[4,728,256]{2,1,0:T(8,128)(2,1)} %constant.19.clone.refs_3_, ...), custom_call_target="tpu_custom_call" | custom-call | tf_op jit(solution)/shard_map/pallas_call | solution.py:428
  63.2 1.3 %copy.18 = f32[1,2,12,6]{2,1,3,0:T(2,128)} copy(f32[1,2,12,6]{2,1,3,0:T(2,128)} %bitcast.19) | data formatting | bytes 1152
  64.5 1.8 %copy.19 = f32[64,13,7,7]{0,3,2,1:T(8,128)} copy(f32[64,13,7,7]{0,3,2,1:T(8,128)} %bitcast.15) | data formatting | bytes 326144
  66.3 1.4 %copy.20 = f32[64,128]{1,0:T(8,128)} copy(f32[64,128]{1,0:T(8,128)} %get-tuple-element.14) | data formatting | bytes 65536

commit v3 on v2

--- a/solution.py
+++ b/solution.py
@@ -12,7 +12,7 @@
 CELL = 8
 TEMP = 0.2
 EPS = 1e-06
-STEP = 4
+STEP = 24
 LANES = 128
 HALF = 64
 

time: 67.9 us -> 53.3 us (0.78)
  Pallas kernels: 60.9 us -> 46.3 us
    pallas_call x1, Pallas kernels: 60.9 us -> 46.3 us  [local(): pl.pallas_call(functools.partial(kernel, (tiles, bands, height, width, n_...]
where the time goes in v3:
time: 53.3 us; the launch traced here: 53 us
  Pallas kernels  46.3 us (87%)
  local copies, waits for them, and re-layouts  6.06 us (11%)
  between operations  0.64 us (1%)
    pallas_call x1, Pallas kernels, local(): pl.pallas_call(functools.partial(kernel, (tiles, bands, height, width, n_...  46.3 us
    unnamed x3, local copies, waits for them, and re-layouts  4.41 us
    pad x1, local copies, waits for them, and re-layouts, local(): jnp.pad(jnp.transpose(w_stem, (1, 2, 3, 0)), ((0, 0), (0, 0), (0, 1), (0,...  1.65 us

profile of v3, /device:TPU:0, one launch (start us, length us, event | category | flops | bytes accessed | tf_op | source)
XLA Modules:
  0.0 53.0 jit_solution(1838961835114507840)
XLA Ops:
  0.6 1.6 %pad.4 = bf16[13,7,8,64]{3,2,1,0:T(8,128)(2,1)} pad(bf16[13,7,7,64]{3,2,1,0:T(8,128)(2,1)} %bitcast.16, bf16[]{:T(256)} %constant.14.clone.1), padding=0_0x0_0x0_1x0_0 | pad | bytes 174722 | tf_op jit(solution)/shard_map/jit(_pad)/pad | solution.py:413
  2.3 46.3 %shard_map.139 = (f32[6,2,12]{2,1,0:T(2,128)}, f32[13,7,7,64]{3,2,1,0:T(8,128)}, f32[64,128]{1,0:T(8,128)}) custom-call(bf16[2,13,192,96]{3,2,1,0:T(8,128)(2,1)} %bitcast.13, bf16[2,32,96]{2,1,0:T(8,128)(2,1)} %constant.16.clone.refs_1_, bf16[728,64]{1,0:T(8,128)(2,1)} %bitcast.14, bf16[4,728,256]{2,1,0:T(8,128)(2,1)} %constant.19.clone.refs_3_, ...), custom_call_target="tpu_custom_call" | custom-call | tf_op jit(solution)/shard_map/pallas_call | solution.py:428
  48.6 1.3 %copy.18 = f32[1,2,12,6]{2,1,3,0:T(2,128)} copy(f32[1,2,12,6]{2,1,3,0:T(2,128)} %bitcast.19) | data formatting | bytes 1152
  49.8 1.8 %copy.19 = f32[64,13,7,7]{0,3,2,1:T(8,128)} copy(f32[64,13,7,7]{0,3,2,1:T(8,128)} %bitcast.15) | data formatting | bytes 326144
  51.6 1.4 %copy.20 = f32[64,128]{1,0:T(8,128)} copy(f32[64,128]{1,0:T(8,128)} %get-tuple-element.14) | data formatting | bytes 65536
